TPU v7x, 512 devices: a whole 4x8x8 slice. The times are simulated.
512 devices in a mesh: seq: 64 (over z_hi, y, core), head: 8 (over x, z_lo).
Axes of the slice: x: 4, y: 8, z: 8 (z_hi: 4, z_lo: 2; z = z_hi * 2 + z_lo), core: 2. Of those that a mesh axis runs over, the one named last changes fastest.
Arguments:
- tokens: bfloat16 [8192, 2880], P('seq'), may hold values from -80 to 80
- gain: float32 [2880], replicated, may hold values from 0.1 to 1.9
- w_query: bfloat16 [2880, 4096], P('seq', 'head'), may hold values from -4 to 4
- w_key: bfloat16 [2880, 512], P('seq', 'head'), may hold values from -1 to 1
- w_value: bfloat16 [2880, 512], P('seq', 'head'), may hold values from -0.109375 to 0.109375
- w_out: bfloat16 [2880, 4096], P('seq', 'head'), may hold values from -0.09375 to 0.09375
- w_gate: float32 [2880], replicated, may hold values from -0.109375 to 0.109375
- steering: bfloat16 [16, 2880], replicated, may hold values from -5 to 5
- segment_ids: int32 [8192], P('seq'), may hold values from 0 to 31, never falling along the last dimension, each value on 1 to 512 neighbouring positions
- steer_index: int32 [8192], P('seq'), may hold values from 0 to 15
- grad_out: bfloat16 [8192, 2880], P('seq'), may hold values from -6 to 6
Outputs:
- layer_out: bfloat16 [8192, 2880], P('seq', 'head')
- grad_tokens: bfloat16 [8192, 2880], P('seq', 'head')
- steer_grad: float32 [16, 2880], P(None, 'head')
Inputs may be any that keep to these rules, and one draw needn't show every extreme that they name: `segment_ids`: the ids never fall along the tokens; each id names one packed document of at most 512 tokens.
All inputs are finite; a program needn't handle non-finite values.
Results may differ from a plain program's by a relative error of at most 0.011.
Values may be sent and summed in bfloat16 or wider, within the bound.
No kernel may reach another device: no remote copies, remote signals or barrier semaphores. Data moves between devices by JAX's collectives and lax.ppermute only.
A program may use at most 64 MiB of HBM per device.

v0:
```python
import jax
import jax.numpy as jnp
from jax import lax
from jax.sharding import Mesh, PartitionSpec as P

HD = 64
WIN = 128
EPSILON = 1e-05
HIGHEST = lax.Precision.HIGHEST
SEQ = ("zh", "y", "core")
HEAD = ("x", "zl")
F32 = jnp.float32
BF16 = jnp.bfloat16
PAD = 48


def shifted(value, by):
    count = lax.axis_size(SEQ)
    pairs = [(i, i + by) for i in range(count) if 0 <= i + by < count]
    return lax.ppermute(value, SEQ, pairs)


def gathered(value, axes):
    count = lax.axis_size(axes)
    spread = jnp.broadcast_to(value[None], (count,) + value.shape)
    return lax.all_to_all(spread, axes, 0, 0)


def dot(left, right, dims, **kw):
    return lax.dot_general(left, right, (dims, ((), ())), preferred_element_type=F32, **kw)


def blocked(rows):
    width = rows.shape[-1]
    parts = rows.reshape(4, 8, 2, -1, width).transpose(1, 0, 2, 3, 4)
    parts = jnp.pad(parts, ((0, 0), (0, 0), (0, 0), (0, PAD - parts.shape[3]), (0, 0)))
    return parts.reshape(-1, width)


def for_heads(rows):
    width = rows.shape[-1]
    parts = rows.reshape(2, 4, 4, 2, PAD, width).transpose(2, 0, 1, 3, 4, 5)
    return parts.reshape(8, -1, width)


def unpadded(rows, row_count):
    width = rows.shape[-1]
    return rows.reshape(8, PAD, width)[:, : row_count // 8].reshape(row_count, width)


def split3(value):
    high = lax.reduce_precision(value, 8, 7)
    rest = value - high
    mid = lax.reduce_precision(rest, 8, 7)
    low = lax.reduce_precision(rest - mid, 8, 7)
    return jnp.stack([high, mid, low])


def shards(
    tokens,
    gain,
    w_query,
    w_key,
    w_value,
    w_out,
    w_gate,
    steering,
    segment_ids,
    steer_index,
    grad_out,
):
    row_count, model_width = tokens.shape
    share = model_width // 8
    start = lax.axis_index(HEAD) * share
    padded = lambda w: jnp.pad(w, ((0, PAD - w.shape[0]), (0, 0)))
    both = jnp.stack([padded(w_query), padded(w_out)])
    half = both.shape[2] // 2
    both = both.reshape(2, PAD, 2, half).transpose(2, 0, 1, 3)
    sent = jnp.broadcast_to(both[None], (4,) + both.shape).reshape((8,) + both.shape[1:])
    near = lax.all_to_all(sent, ("zh", "core"), 0, 0)
    q_own = lax.all_gather(near[:, 0], "y", axis=0, tiled=True).reshape(-1, half)
    o_own = lax.all_gather(near[:, 1], "y", axis=0, tiled=True).reshape(-1, half)
    w_kv = padded(jnp.concatenate([w_key, w_value], axis=1))
    kv_near = lax.all_gather(w_kv, ("zh",), axis=0, tiled=False)
    kv_all = lax.all_gather(kv_near, ("y", "core"), axis=0, tiled=False)
    kv_all = kv_all.reshape(8, 2, 4, PAD, 2 * HD).transpose(0, 2, 1, 3, 4).reshape(-1, 2 * HD)
    flip = [(0, 1), (1, 0)]
    q_oth = lax.ppermute(q_own, "core", flip)
    o_oth = lax.ppermute(o_own, "core", flip)
    tok = tokens.T.astype(F32)
    inverse = lax.rsqrt(jnp.mean(tok * tok, axis=0, keepdims=True) + EPSILON)
    unit = tok * inverse
    normed = (unit * gain[:, None]).astype(BF16)
    normed_b = blocked(normed)
    unit_b = blocked(unit * gain[:, None])
    grad_t = grad_out.T
    grad_b = blocked(grad_t)
    gate = jax.nn.sigmoid(jnp.sum(normed.astype(F32) * w_gate[:, None], axis=0))
    one_hot = steer_index[None, :] == lax.broadcasted_iota(jnp.int32, (16, row_count), 0)
    products = dot(steering, grad_t, ((1,), (0,)))
    grad_logit = gate * (1.0 - gate) * jnp.sum(jnp.where(one_hot, products, 0.0), axis=0)
    steer_share = lax.dynamic_slice_in_dim(steering, start, share, 1)
    steer_rows = dot(steer_share, one_hot.astype(BF16), ((0,), (0,)))
    grad_share = lax.dynamic_slice_in_dim(grad_t, start, share, 0).astype(F32)
    steer_part = dot(
        one_hot.astype(F32), gate[None, :] * grad_share, ((1,), (1,)), precision=HIGHEST
    )
    steer_near = jnp.sum(gathered(steer_part, ("zh", "core")), axis=0)
    steer_grad = jnp.sum(gathered(steer_near, ("y",)), axis=0)
    halo_seg = shifted(segment_ids, 1)
    halo_seg = jnp.where(lax.axis_index(SEQ) > 0, halo_seg, -1)
    kv = dot(kv_all, normed_b, ((0,), (0,))).astype(BF16)
    kv_halo = shifted(kv, 1)
    wide = jnp.concatenate([kv_halo, kv], axis=1)
    keys, values = (wide[:HD], wide[HD:])
    wide_seg = jnp.concatenate([halo_seg, segment_ids])
    query_pos = lax.broadcasted_iota(jnp.int32, (row_count, 2 * row_count), 0)
    key_pos = lax.broadcasted_iota(jnp.int32, (row_count, 2 * row_count), 1) - WIN
    distance = query_pos - key_pos
    mask = (distance >= 0) & (distance < WIN) & (segment_ids[:, None] == wide_seg[None, :])
    query = jnp.concatenate(
        [
            dot(q_own, normed_b, ((0,), (0,))).astype(BF16),
            dot(q_oth, normed_b, ((0,), (0,))).astype(BF16),
        ]
    ).reshape(8, HD, row_count)
    scores = jnp.einsum("hdq,dk->hqk", query, keys, preferred_element_type=F32) * HD ** (-0.5)
    scores = jnp.where(mask[None], scores, -jnp.inf)
    raised = jnp.exp(scores - jnp.max(scores, axis=-1, keepdims=True))
    probs = raised / jnp.sum(raised, axis=-1, keepdims=True)
    probs_b = probs.astype(BF16)
    mixed = jnp.einsum("hqk,dk->hdq", probs_b, values, preferred_element_type=F32)
    mixed = mixed.astype(BF16).reshape(2, half, row_count)
    term = dot(o_own, mixed[0], ((1,), (0,))) + dot(o_oth, mixed[1], ((1,), (0,)))
    attn = lax.all_to_all(for_heads(term.astype(BF16)), HEAD, 0, 0)
    attn_share = unpadded(jnp.sum(attn.astype(F32), axis=0), share)
    token_share = lax.dynamic_slice_in_dim(tokens.T, start, share, 0).astype(F32)
    layer_out = (token_share + attn_share + gate[None, :] * steer_rows).astype(BF16)
    grad_mixed = jnp.concatenate(
        [
            dot(o_own, grad_b, ((0,), (0,))).astype(BF16),
            dot(o_oth, grad_b, ((0,), (0,))).astype(BF16),
        ]
    ).reshape(8, HD, row_count)
    grad_values = jnp.einsum("hqk,hdq->dk", probs_b, grad_mixed, preferred_element_type=F32)
    grad_prob = jnp.einsum("hdq,dk->hqk", grad_mixed, values, preferred_element_type=F32)
    delta = jnp.sum(probs * grad_prob, axis=-1, keepdims=True)
    grad_scores = (probs * (grad_prob - delta) * HD ** (-0.5)).astype(BF16)
    grad_query = jnp.einsum("hqk,dk->hdq", grad_scores, keys, preferred_element_type=F32)
    grad_query = grad_query.astype(BF16).reshape(2, half, row_count)
    grad_keys = jnp.einsum("hqk,hdq->dk", grad_scores, query, preferred_element_type=F32)
    grad_kv = jnp.concatenate([grad_keys, grad_values])
    returned = shifted(grad_kv[:, :WIN].astype(BF16), -1)
    grad_kv = (grad_kv[:, WIN:] + returned.astype(F32)).astype(BF16)
    terms = (
        dot(q_own, grad_query[0], ((1,), (0,)))
        + dot(q_oth, grad_query[1], ((1,), (0,)))
        + dot(kv_all, grad_kv, ((1,), (0,)))
    ).astype(BF16)
    row_part = split3(jnp.sum(terms.astype(F32) * unit_b, axis=0)).astype(BF16)
    extra = jnp.broadcast_to(jnp.pad(row_part, ((0, 13), (0, 0)))[None], (8, 16, row_count))
    back = lax.all_to_all(jnp.concatenate([for_heads(terms), extra], axis=1), HEAD, 0, 0)
    back = jnp.sum(back.astype(F32), axis=0)
    gain_share = lax.dynamic_slice_in_dim(gain, start, share, 0)[:, None]
    gate_share = lax.dynamic_slice_in_dim(w_gate, start, share, 0)[:, None]
    total = unpadded(back[: 8 * PAD], share) + grad_logit[None, :] * gate_share
    gate_total = jnp.sum(unit * (gain * w_gate)[:, None], axis=0)
    row_total = jnp.sum(back[8 * PAD : 8 * PAD + 3], axis=0) + grad_logit * gate_total
    unit_share = token_share * inverse
    scaled = total * gain_share
    grad_tokens = (
        grad_share + inverse * (scaled - unit_share * (row_total / model_width)[None, :])
    ).astype(BF16)
    return (layer_out.T, grad_tokens.T, steer_grad)


def solution(mesh):
    split = Mesh(mesh.devices.reshape(4, 8, 2, 4, 2), SEQ + HEAD)
    placed = (
        P(SEQ, None),
        P(),
        P(SEQ, HEAD),
        P(SEQ, HEAD),
        P(SEQ, HEAD),
        P(SEQ, HEAD),
        P(),
        P(),
        P(SEQ),
        P(SEQ),
        P(SEQ, None),
    )
    return jax.shard_map(
        shards,
        mesh=split,
        in_specs=placed,
        out_specs=(P(SEQ, HEAD), P(SEQ, HEAD), P(None, HEAD)),
        check_vma=False,
    )
```

profile of v0, /device:TPU:2, one launch (start us, length us, event | category | flops | bytes accessed | tf_op | source)
XLA Modules:
  0.0 241.0 jit_solution(13641125180174731504)
XLA Ops:
  7.2 0.8 pad.26
  8.1 0.9 pad.27
  9.2 25.7 %all_to_all.25 = bf16[8,2,48,256]{3,2,1,0:T(8,128)(2,1)S(1)} all-to-all(bf16[8,2,48,256]{3,2,1,0:T(8,128)(2,1)S(1)} %bitcast.165), channel_id=1, replica_groups=mesh['zh'=4,'y'=8,'core'=2,'x'=4,'zl'=2] {'zh','core'}, dimensions={0} | all-to-all | bytes 786432 | tf_op jit(solution)/shard_map/all_to_all | solution.py:80
  34.9 0.8 fusion.104
  35.7 0.7 all-gather.9.cloned.1.call-update
  36.4 1.9 collective-permute-start.1
  38.7 1.5 multiply_reduce_fusion
  41.1 13.8 %all-gather.1 = bf16[192,128]{1,0:T(8,128)(2,1)S(1)} all-gather(bf16[48,128]{1,0:T(8,128)(2,1)S(1)} %fusion.63), channel_id=3, replica_groups=mesh['zh'=4,'y'=8,'core'=2,'x'=4,'zl'=2] {'zh'}, dimensions={0}, use_global_device_ids=true | all-gather | bytes 61440 | tf_op jit(solution)/shard_map/all_gather | solution.py:84
  54.8 22.2 %all-gather.2 = bf16[64,48,128]{2,1,0:T(8,128)(2,1)S(1)} all-gather(bf16[4,48,128]{2,1,0:T(8,128)(2,1)S(1)} %bitcast.174), channel_id=4, replica_groups=mesh['zh'=4,'y'=8,'core'=2,'x'=4,'zl'=2] {'y','core'}, dimensions={0}, use_global_device_ids=true | all-gather | bytes 835584 | tf_op jit(solution)/shard_map/all_gather | solution.py:85
  77.1 2.2 collective-permute-start.3
  79.8 2.1 collective-permute-start
  81.8 3.2 %fusion.10 = (f32[128]{0:T(128)}, f32[2880,128]{1,0:T(8,128)}) fusion(bf16[128,2880]{0,1:T(8,128)(2,1)S(1)} %copy-done.1, f32[2880]{0:T(1024)S(1)} %mul.187, f32[128]{0:T(128)S(1)} %add_rsqrt_fusion, f32[2880]{0:T(1024)S(1)} %copy-done.13), kind=kLoop, calls=%fused_computation.17 | loop fusion | flops 1843072 | bytes 2235904 | tf_op jit(solution)/shard_map/reduce_sum | solution.py:167
  85.1 33.8 %all-gather.9.cloned.1.call-done = bf16[64,1,48,256]{3,2,1,0:T(8,128)(2,1)} async-done(((bf16[8,1,48,256]{3,2,1,0:T(8,128)(2,1)}), bf16[64,1,48,256]{3,2,1,0:T(8,128)(2,1)}) %all-gather.9.cloned.1.call-update) | async-done | bytes 1572880 | tf_op jit(solution)/shard_map/all_gather | solution.py:81
  118.8 2.0 collective-permute-start.2
  121.0 0.9 copy.43
  122.5 2.5 %reshape.221 = f32[4,8,2,45,128]{4,3,2,1,0:T(8,128)} reshape(f32[2880,128]{1,0:T(8,128)} %get-tuple-element.9) | data formatting | bytes 2949120 | tf_op jit(solution)/shard_map/reshape | solution.py:35
  125.0 2.8 %copy.63 = f32[8,4,2,45,128]{4,3,2,1,0:T(8,128)} copy(f32[8,4,2,45,128]{4,3,2,0,1:T(8,128)} %bitcast.154) | data formatting | bytes 2949120
  127.8 2.8 %pad.31.clone = f32[8,4,2,48,128]{4,3,2,1,0:T(8,128)} pad(f32[8,4,2,45,128]{4,3,2,1,0:T(8,128)} %copy.63, f32[]{:T(128)} %constant.42.clone.1), padding=0_0x0_0x0_0x0_3x0_0 | pad | bytes 3047428 | tf_op jit(solution)/shard_map/jit(_pad)/pad | solution.py:36
  130.7 0.6 convolution_convert_fusion.5
  131.3 0.6 copy-done.2
  132.6 2.0 convolution_convert_fusion.2
  134.7 2.0 convolution_convert_fusion.4
  137.1 1.6 fusion.107
  138.8 7.2 %convolution_bitcast_fusion.2 = f32[64,256]{1,0:T(8,128)S(1)} fusion(bf16[8,64,128]{2,1,0:T(8,128)(2,1)S(1)} %bitcast.176, f32[8,128,256]{2,1,0:T(8,128)S(1)} %fusion.65, f32[8,128,256]{2,1,0:T(8,128)} %get-tuple-element.20, f32[8,128]{1,0:T(8,128)S(1)} %get-tuple-element.19), kind=kOutput, calls=%fused_computation.41 | convolution fusion | flops 35390720 | bytes 2297856 | tf_op jit(solution)/shard_map/hqk,hdq->dk/dot_general | solution.py:151
  146.0 7.3 %fusion.21 = bf16[8,64,128]{2,1,0:T(8,128)(2,1)S(1)} fusion(f32[8,128,256]{2,1,0:T(8,128)S(1)} %fusion.65, bf16[128,128]{0,1:T(8,128)(2,1)S(1)} %fusion.23, bf16[128,128]{0,1:T(8,128)(2,1)S(1)} %collective-permute-done, f32[8,128,256]{2,1,0:T(8,128)} %get-tuple-element.20, f32[8,128]{1,0:T(8,128)S(1)} %get-tuple-element.19), kind=kOutput, calls=%fused_computation.33 | convolution fusion | flops 35521792 | bytes 2297856 | tf_op jit(solution)/shard_map/hqk,dk->hdq/dot_general | solution.py:149
  153.3 3.0 %convolution_bitcast_fusion.1 = f32[64,256]{1,0:T(8,128)S(1)} fusion(bf16[8,64,128]{2,1,0:T(8,128)(2,1)S(1)} %bitcast.169, f32[8,128]{1,0:T(8,128)} %copy-done.25, bf16[8,64,128]{2,1,0:T(8,128)(2,1)} %bitcast.177, pred[128,256]{1,0:T(8,128)(4,1)} %copy-done.19, bf16[128,128]{0,1:T(8,128)(2,1)} %copy-done.15, bf16[128,128]{0,1:T(8,128)(2,1)} %copy-done.17), kind=kOutput, calls=%fused_computation.40 | convolution fusion | flops 68486400 | bytes 430080 | tf_op jit(solution)/shard_map/hqk,hdq->dk/dot_general | solution.py:145
  156.4 1.5 collective-permute-start.4
  158.5 1.0 collective-permute-done.4
  159.9 2.3 fusion.7
  162.4 0.9 pad_maximum_fusion
  163.3 5.9 %all-to-all-start.2 = ((bf16[8,400,128]{2,1,0:T(8,128)(2,1)}), bf16[8,400,128]{2,1,0:T(8,128)(2,1)}, u32[]{:S(2)}, u32[]{:S(2)}) async-start(bf16[8,400,128]{2,1,0:T(8,128)(2,1)} %pad_maximum_fusion), calls=%async_computation.2 | async-start | bytes 1638400 | tf_op jit(solution)/shard_map/all_to_all | solution.py:162
  169.2 3.0 %fusion.20 = bf16[8,64,128]{2,1,0:T(8,128)(2,1)S(1)} fusion(bf16[128,128]{0,1:T(8,128)(2,1)S(1)} %copy-done.16, bf16[128,128]{0,1:T(8,128)(2,1)S(1)} %copy-done.18, f32[8,128]{1,0:T(8,128)S(1)} %copy-done.26, bf16[8,64,128]{2,1,0:T(8,128)(2,1)S(1)} %bitcast.178, pred[128,256]{1,0:T(8,128)(4,1)} %copy-done.19), kind=kOutput, calls=%fused_computation.32 | convolution fusion | flops 68617472 | bytes 430080 | tf_op jit(solution)/shard_map/hqk,dk->hdq/dot_general | solution.py:132
  172.9 2.0 fusion.3
  174.9 1.0 copy.47
  175.8 4.1 %all-to-all-done.2 = bf16[8,400,128]{2,1,0:T(8,128)(2,1)} async-done(((bf16[8,400,128]{2,1,0:T(8,128)(2,1)}), bf16[8,400,128]{2,1,0:T(8,128)(2,1)}, u32[]{:S(2)}, u32[]{:S(2)}) %all-to-all-start.2) | async-done | bytes 819232 | tf_op jit(solution)/shard_map/all_to_all | solution.py:162
  180.0 6.7 %all-to-all-start.1 = ((bf16[8,384,128]{2,1,0:T(8,128)(2,1)}), bf16[8,384,128]{2,1,0:T(8,128)(2,1)S(1)}, u32[]{:S(2)}, u32[]{:S(2)}) async-start(bf16[8,384,128]{2,1,0:T(8,128)(2,1)} %bitcast.21), calls=%async_computation.1 | async-start | bytes 1572864 | tf_op jit(solution)/shard_map/all_to_all | solution.py:135
  186.9 1.3 convert_reduce_fusion
  188.4 10.4 %all-to-all-done.1 = bf16[8,384,128]{2,1,0:T(8,128)(2,1)S(1)} async-done(((bf16[8,384,128]{2,1,0:T(8,128)(2,1)}), bf16[8,384,128]{2,1,0:T(8,128)(2,1)S(1)}, u32[]{:S(2)}, u32[]{:S(2)}) %all-to-all-start.1) | async-done | bytes 786464 | tf_op jit(solution)/shard_map/all_to_all | solution.py:135
  198.9 0.7 broadcast_in_dim.34
  199.5 6.0 %all-to-all-start.3 = ((f32[8,16,360]{2,1,0:T(8,128)}), f32[8,16,360]{2,1,0:T(8,128)S(1)}, u32[]{:S(2)}, u32[]{:S(2)}) async-start(f32[8,16,360]{2,1,0:T(8,128)} %broadcast_in_dim.34), calls=%async_computation.3 | async-start | bytes 393216 | tf_op jit(solution)/shard_map/all_to_all | solution.py:26
  205.6 0.8 dynamic_slice.18
  206.6 10.4 %all-to-all-done.3 = f32[8,16,360]{2,1,0:T(8,128)S(1)} async-done(((f32[8,16,360]{2,1,0:T(8,128)}), f32[8,16,360]{2,1,0:T(8,128)S(1)}, u32[]{:S(2)}, u32[]{:S(2)}) %all-to-all-start.3) | async-done | bytes 184352 | tf_op jit(solution)/shard_map/all_to_all | solution.py:26
  217.0 0.7 broadcast_in_dim.35
  217.6 6.1 %all-to-all-start.4 = ((f32[8,16,360]{2,1,0:T(8,128)}), f32[8,16,360]{2,1,0:T(8,128)S(1)}, u32[]{:S(2)}, u32[]{:S(2)}) async-start(f32[8,16,360]{2,1,0:T(8,128)} %broadcast_in_dim.35), calls=%async_computation.4 | async-start | bytes 393216 | tf_op jit(solution)/shard_map/all_to_all | solution.py:26
  223.7 1.0 fusion.22
  224.7 0.8 fusion.44
  225.5 8.0 %all-to-all-done.4 = f32[8,16,360]{2,1,0:T(8,128)S(1)} async-done(((f32[8,16,360]{2,1,0:T(8,128)}), f32[8,16,360]{2,1,0:T(8,128)S(1)}, u32[]{:S(2)}, u32[]{:S(2)}) %all-to-all-start.4) | async-done | bytes 184352 | tf_op jit(solution)/shard_map/all_to_all | solution.py:26
  233.5 0.6 reduce_sum.122
  (105 shorter events, 6.2 us)
Async XLA Ops:
  7.2 179.5 %copy-start = (bf16[16,2880]{1,0:T(8,128)(2,1)S(1)}, bf16[16,2880]{1,0:T(8,128)(2,1)}, u32[]{:S(2)}) copy-start(bf16[16,2880]{1,0:T(8,128)(2,1)} %param.18) | copy-start | bytes 276484
  7.2 69.9 %all-gather.7.cloned.1.call-start = ((), (), s32[]{:S(2)}) async-start(), calls=%async_computation.5 | async-start | bytes 1769472 | tf_op jit(solution)/shard_map/all_gather | solution.py:82
  8.0 28.4 %copy-start.23 = (s32[128]{0:T(128)S(1)}, s32[128]{0:T(128)}, u32[]{:S(2)}) copy-start(s32[128]{0:T(128)} %param.19) | copy-start | bytes 1540
  8.0 30.3 %copy-start.1 = (bf16[128,2880]{0,1:T(8,128)(2,1)S(1)}, bf16[128,2880]{0,1:T(8,128)(2,1)}, u32[]{:S(2)}) copy-start(bf16[128,2880]{0,1:T(8,128)(2,1)} %param.11) | copy-start | bytes 2211844
  9.1 29.6 %copy-start.13 = (f32[2880]{0:T(1024)S(1)}, f32[2880]{0:T(1024)}, u32[]{:S(2)}) copy-start(f32[2880]{0:T(1024)} %param.12) | copy-start | bytes 34564
  9.1 29.6 %copy-start.14 = (f32[2880]{0:T(1024)S(1)}, f32[2880]{0:T(1024)}, u32[]{:S(2)}) copy-start(f32[2880]{0:T(1024)} %param.17) | copy-start | bytes 34564
  35.7 83.2 %all-gather.9.cloned.1.call-start = ((), (), s32[]{:S(2)}) async-start(), calls=%async_computation.6 | async-start | bytes 1769472 | tf_op jit(solution)/shard_map/all_gather | solution.py:81
  36.4 94.1 %collective-permute-start.1 = (s32[128]{0:T(128)S(1)}, s32[128]{0:T(128)S(1)}, u32[]{:S(2)}, u32[]{:S(2)}) collective-permute-start(s32[128]{0:T(128)S(1)} %copy-done.23), channel_id=1, source_target_pairs={{0,8},{8,16},{16,24},{24,32},{32,40},{40,48},{48,56},{56,64},{64,7... | collective-permute-start | bytes 1544 | tf_op jit(solution)/shard_map/ppermute | solution.py:20
  40.3 0.7 copy-start.20
  40.3 0.7 copy-start.21
  77.1 8.0 %copy-start.9 = (bf16[64,48,128]{2,1,0:T(8,128)(2,1)}, bf16[64,48,128]{2,1,0:T(8,128)(2,1)S(1)}, u32[]{:S(2)}) copy-start(bf16[64,48,128]{2,1,0:T(8,128)(2,1)S(1)} %all-gather.2) | copy-start | bytes 2359300
  77.1 55.5 %collective-permute-start.3 = (bf16[3072,256]{1,0:T(8,128)(2,1)}, bf16[3072,256]{1,0:T(8,128)(2,1)}, u32[]{:S(2)}, u32[]{:S(2)}) collective-permute-start(bf16[3072,256]{1,0:T(8,128)(2,1)} %bitcast.148), channel_id=1, source_target_pairs={{0,8},{8,0},{1,9},{9,1},{2,10},{10,2},{3,11},{11,3},{4,12},{12,4},... | collective-permute-start | bytes 4718600 | tf_op jit(solution)/shard_map/ppermute | solution.py:89
  79.7 66.2 %copy-start.15 = (bf16[128,128]{0,1:T(8,128)(2,1)}, bf16[128,128]{0,1:T(8,128)(2,1)S(1)}, u32[]{:S(2)}) copy-start(bf16[128,128]{0,1:T(8,128)(2,1)S(1)} %fusion.23) | copy-start | bytes 98308
  79.8 57.0 %collective-permute-start = (bf16[128,128]{0,1:T(8,128)(2,1)S(1)}, bf16[128,128]{0,1:T(8,128)(2,1)S(1)}, u32[]{:S(2)}, u32[]{:S(2)}) collective-permute-start(bf16[128,128]{0,1:T(8,128)(2,1)S(1)} %fusion.23), channel_id=1, source_target_pairs={{0,8},{8,16},{16,24},{24,32},{32,40},{40,48},{48,56},{56,64},{64,7... | collective-permute-start | bytes 98312 | tf_op jit(solution)/shard_map/ppermute | solution.py:20
  118.8 2.2 copy-start.10
  118.8 15.8 %collective-permute-start.2 = (bf16[3072,256]{1,0:T(8,128)(2,1)}, bf16[3072,256]{1,0:T(8,128)(2,1)}, u32[]{:S(2)}, u32[]{:S(2)}) collective-permute-start(bf16[3072,256]{1,0:T(8,128)(2,1)} %bitcast.151), channel_id=1, source_target_pairs={{0,8},{8,0},{1,9},{9,1},{2,10},{10,2},{3,11},{11,3},{4,12},{12,4},... | collective-permute-start | bytes 4718600 | tf_op jit(solution)/shard_map/ppermute | solution.py:88
  120.9 1.2 copy-start.7
  127.8 2.9 %copy-start.4 = (bf16[64,1,48,256]{3,2,1,0:T(8,128)(2,1)S(1)}, bf16[64,1,48,256]{3,2,1,0:T(8,128)(2,1)}, u32[]{:S(2)}) copy-start(bf16[64,1,48,256]{3,2,1,0:T(8,128)(2,1)} %all-gather.9.cloned.1.call-done) | copy-start | bytes 4718596
  130.6 1.4 copy-start.2
  130.7 6.4 %copy-start.19 = (pred[128,256]{1,0:T(8,128)(4,1)}, pred[128,256]{1,0:T(8,128)(4,1)S(1)}, u32[]{:S(2)}) copy-start(pred[128,256]{1,0:T(8,128)(4,1)S(1)} %fusion.43) | copy-start | bytes 98308
  136.7 16.6 %copy-start.11 = (bf16[512,128]{1,0:T(8,128)(2,1)}, bf16[512,128]{1,0:T(8,128)(2,1)S(1)}, u32[]{:S(2)}) copy-start(bf16[512,128]{1,0:T(8,128)(2,1)S(1)} %pad_maximum_fusion.1) | copy-start | bytes 393220
  136.7 9.2 %copy-start.17 = (bf16[128,128]{0,1:T(8,128)(2,1)}, bf16[128,128]{0,1:T(8,128)(2,1)S(1)}, u32[]{:S(2)}) copy-start(bf16[128,128]{0,1:T(8,128)(2,1)S(1)} %collective-permute-done) | copy-start | bytes 98308
  138.8 7.2 %copy-start.25 = (f32[8,128]{1,0:T(8,128)}, f32[8,128]{1,0:T(8,128)S(1)}, u32[]{:S(2)}) copy-start(f32[8,128]{1,0:T(8,128)S(1)} %get-tuple-element.19) | copy-start | bytes 12292
  153.3 4.5 %copy-start.5 = (bf16[64,1,48,256]{3,2,1,0:T(8,128)(2,1)S(1)}, bf16[64,1,48,256]{3,2,1,0:T(8,128)(2,1)}, u32[]{:S(2)}) copy-start(bf16[64,1,48,256]{3,2,1,0:T(8,128)(2,1)} %all-gather.9.cloned.1.call-done) | copy-start | bytes 4718596
  156.4 3.1 %collective-permute-start.4 = (bf16[128,128]{1,0:T(8,128)(2,1)S(1)}, bf16[128,128]{1,0:T(8,128)(2,1)S(1)}, u32[]{:S(2)}, u32[]{:S(2)}) collective-permute-start(bf16[128,128]{1,0:T(8,128)(2,1)S(1)} %fusion.50), channel_id=1, source_target_pairs={{8,0},{16,8},{24,16},{32,24},{40,32},{48,40},{56,48},{64,56},{72,6... | collective-permute-start | bytes 98312 | tf_op jit(solution)/shard_map/ppermute | solution.py:20
  157.9 1.6 copy-start.8
  158.4 1.5 copy-start.6
  162.3 6.9 %copy-start.12 = (bf16[512,128]{1,0:T(8,128)(2,1)S(1)}, bf16[512,128]{1,0:T(8,128)(2,1)}, u32[]{:S(2)}) copy-start(bf16[512,128]{1,0:T(8,128)(2,1)} %copy-done.11) | copy-start | bytes 393220
  162.3 6.9 %copy-start.16 = (bf16[128,128]{0,1:T(8,128)(2,1)S(1)}, bf16[128,128]{0,1:T(8,128)(2,1)}, u32[]{:S(2)}) copy-start(bf16[128,128]{0,1:T(8,128)(2,1)} %copy-done.15) | copy-start | bytes 98308
  162.3 6.9 %copy-start.18 = (bf16[128,128]{0,1:T(8,128)(2,1)S(1)}, bf16[128,128]{0,1:T(8,128)(2,1)}, u32[]{:S(2)}) copy-start(bf16[128,128]{0,1:T(8,128)(2,1)} %copy-done.17) | copy-start | bytes 98308
  162.4 6.9 %copy-start.26 = (f32[8,128]{1,0:T(8,128)S(1)}, f32[8,128]{1,0:T(8,128)}, u32[]{:S(2)}) copy-start(f32[8,128]{1,0:T(8,128)} %copy-done.25) | copy-start | bytes 12292
  163.3 16.6 %all-to-all-start.2 = ((bf16[8,400,128]{2,1,0:T(8,128)(2,1)}), bf16[8,400,128]{2,1,0:T(8,128)(2,1)}, u32[]{:S(2)}, u32[]{:S(2)}) async-start(bf16[8,400,128]{2,1,0:T(8,128)(2,1)} %pad_maximum_fusion), calls=%async_computation.2 | async-start | bytes 1638400 | tf_op jit(solution)/shard_map/all_to_all | solution.py:162
  169.2 3.1 %copy-start.3 = (bf16[64,1,48,256]{3,2,1,0:T(8,128)(2,1)S(1)}, bf16[64,1,48,256]{3,2,1,0:T(8,128)(2,1)}, u32[]{:S(2)}) copy-start(bf16[64,1,48,256]{3,2,1,0:T(8,128)(2,1)} %all-gather.7.cloned.1.call-done) | copy-start | bytes 4718596
  174.8 11.8 %copy-start.22 = (s32[128]{0:T(128)S(1)}, s32[128]{0:T(128)}, u32[]{:S(2)}) copy-start(s32[128]{0:T(128)} %param.20) | copy-start | bytes 1540
  179.9 8.2 %copy-start.24 = (f32[128]{0:T(128)S(1)}, f32[128]{0:T(128)}, u32[]{:S(2)}) copy-start(f32[128]{0:T(128)} %get-tuple-element.8) | copy-start | bytes 1540
  180.0 18.9 %all-to-all-start.1 = ((bf16[8,384,128]{2,1,0:T(8,128)(2,1)}), bf16[8,384,128]{2,1,0:T(8,128)(2,1)S(1)}, u32[]{:S(2)}, u32[]{:S(2)}) async-start(bf16[8,384,128]{2,1,0:T(8,128)(2,1)} %bitcast.21), calls=%async_computation.1 | async-start | bytes 1572864 | tf_op jit(solution)/shard_map/all_to_all | solution.py:135
  199.5 17.4 %all-to-all-start.3 = ((f32[8,16,360]{2,1,0:T(8,128)}), f32[8,16,360]{2,1,0:T(8,128)S(1)}, u32[]{:S(2)}, u32[]{:S(2)}) async-start(f32[8,16,360]{2,1,0:T(8,128)} %broadcast_in_dim.34), calls=%async_computation.3 | async-start | bytes 393216 | tf_op jit(solution)/shard_map/all_to_all | solution.py:26
  217.6 15.8 %all-to-all-start.4 = ((f32[8,16,360]{2,1,0:T(8,128)}), f32[8,16,360]{2,1,0:T(8,128)S(1)}, u32[]{:S(2)}, u32[]{:S(2)}) async-start(f32[8,16,360]{2,1,0:T(8,128)} %broadcast_in_dim.35), calls=%async_computation.4 | async-start | bytes 393216 | tf_op jit(solution)/shard_map/all_to_all | solution.py:26
Sparse Core Ops, SparseCore 0:
  35.8 39.7 all-gather.6
  77.7 41.1 all-gather.8
where the time goes:
time: 242 us; the launch traced here: 241 us
  waiting for transfers between devices  68.4 us (28%)
  blocking collectives  61.7 us (25%)
  matrix products  35.3 us (15%)
  starting transfers between devices  34.4 us (14%)
  local copies, waits for them, and re-layouts  17 us (7%)
  between operations  14.7 us (6%)
  other arithmetic  9.35 us (4%)
    all_gather x1, waiting for transfers between devices, shards(): lax.all_gather(near[:, 0], 'y', axis=0, tiled=True).reshape(-1, half)  33.8 us
    all_to_all x1, blocking collectives, shards(): near = lax.all_to_all(sent, ('zh', 'core'), 0, 0)  25.7 us
    all_gather x1, blocking collectives, shards(): kv_all = lax.all_gather(kv_near, ('y', 'core'), axis=0, tiled=False)  22.2 us
    all_to_all x2, waiting for transfers between devices, gathered(): return lax.all_to_all(spread, axes, 0, 0)  18.3 us
    all_gather x1, blocking collectives, shards(): kv_near = lax.all_gather(w_kv, ('zh',), axis=0, tiled=False)  13.8 us
    dot_general x13, matrix products, dot(): lax.dot_general(left, right, (dims, ((), ())), preferred_element_type=F32...  12.8 us
    all_to_all x2, starting transfers between devices, gathered(): return lax.all_to_all(spread, axes, 0, 0)  12.1 us
    all_to_all x1, waiting for transfers between devices, shards(): attn = lax.all_to_all(for_heads(term.astype(BF16)), HEAD, 0, 0)  10.4 us
  transfers between devices with their start and end apart: 11, of which 6 were waited for; matrix products, arithmetic and copies ran while one was open for 13% of the time, Pallas kernels for 0%

commit v1 on v0

--- a/solution.py
+++ b/solution.py
@@ -78,7 +78,9 @@
     both = both.reshape(2, PAD, 2, half).transpose(2, 0, 1, 3)
     sent = jnp.broadcast_to(both[None], (4,) + both.shape).reshape((8,) + both.shape[1:])
     near = lax.all_to_all(sent, ("zh", "core"), 0, 0)
-    q_own = lax.all_gather(near[:, 0], "y", axis=0, tiled=True).reshape(-1, half)
+    q_own = jnp.concatenate(
+        lax.all_to_all(jnp.stack([near[:, 0]] * lax.axis_size("y")), "y", 0, 0), axis=0
+    ).reshape(-1, half)
     o_own = lax.all_gather(near[:, 1], "y", axis=0, tiled=True).reshape(-1, half)
     w_kv = padded(jnp.concatenate([w_key, w_value], axis=1))
     kv_near = lax.all_gather(w_kv, ("zh",), axis=0, tiled=False)

time: 242 us -> 247 us (1.021)
  waiting for transfers between devices: 68.4 us -> 37.3 us
  blocking collectives: 61.7 us -> 83.6 us
  local copies, waits for them, and re-layouts: 17 us -> 25.5 us
  matrix products: 35.3 us -> 39.8 us
    all_gather x1 -> x0, waiting for transfers between devices: 33.8 us -> none  [shards(): lax.all_gather(near[:, 0], 'y', axis=0, tiled=True).reshape(-1, half)]
    all_gather x1, blocking collectives: 22.2 us -> 44.2 us  [shards(): kv_all = lax.all_gather(kv_near, ('y', 'core'), axis=0, tiled=False)]
    all_to_all x0 -> x1, starting transfers between devices: none -> 7.23 us  [shards(): lax.all_to_all(jnp.stack([near[:, 0]] * lax.axis_size('y')), 'y', 0, 0)]
    all_to_all x2, starting transfers between devices: 12.1 us -> 7.89 us  [gathered(): return lax.all_to_all(spread, axes, 0, 0)]
    reshape x4, local copies, waits for them, and re-layouts: 3.01 us -> 6.92 us  [blocked(): parts = rows.reshape(4, 8, 2, -1, width).transpose(1, 0, 2, 3, 4)]
    unnamed x56 -> x46, local copies, waits for them, and re-layouts: 4.24 us -> 5.44 us
  transfers between devices with their start and end apart: 11 -> 11, of which waited for: 6 -> 4; matrix products, arithmetic and copies ran while one was open for 13% -> 20% of each run, Pallas kernels for 0% -> 0%
where the time goes in v1:
time: 247 us; the launch traced here: 246 us
  blocking collectives  83.6 us (34%)
  matrix products  39.8 us (16%)
  waiting for transfers between devices  37.3 us (15%)
  starting transfers between devices  35.1 us (14%)
  local copies, waits for them, and re-layouts  25.5 us (10%)
  between operations  14.6 us (6%)
  other arithmetic  10.1 us (4%)
    all_gather x1, blocking collectives, shards(): kv_all = lax.all_gather(kv_near, ('y', 'core'), axis=0, tiled=False)  44.2 us
    all_to_all x1, blocking collectives, shards(): near = lax.all_to_all(sent, ('zh', 'core'), 0, 0)  25.7 us
    all_to_all x2, waiting for transfers between devices, gathered(): return lax.all_to_all(spread, axes, 0, 0)  19.7 us
    dot_general x13, matrix products, dot(): lax.dot_general(left, right, (dims, ((), ())), preferred_element_type=F32...  14.7 us
    all_gather x1, blocking collectives, shards(): kv_near = lax.all_gather(w_kv, ('zh',), axis=0, tiled=False)  13.7 us
    all_to_all x1, waiting for transfers between devices, shards(): attn = lax.all_to_all(for_heads(term.astype(BF16)), HEAD, 0, 0)  10.7 us
    all_to_all x2, starting transfers between devices, gathered(): return lax.all_to_all(spread, axes, 0, 0)  7.89 us
    dot_general x1, matrix products, shards(): jnp.einsum('hqk,dk->hdq', grad_scores, keys, preferred_element_type=F32)  7.89 us
  transfers between devices with their start and end apart: 11, of which 4 were waited for; matrix products, arithmetic and copies ran while one was open for 20% of the time, Pallas kernels for 0%

profile of v1, /device:TPU:2, one launch (start us, length us, event | category | flops | bytes accessed | tf_op | source)
XLA Modules:
  0.0 246.0 jit_solution(12845057809641088719)
XLA Ops:
  7.2 0.8 pad.26
  9.1 25.7 %all_to_all.30 = bf16[8,2,48,256]{3,2,1,0:T(8,128)(2,1)S(1)} all-to-all(bf16[8,2,48,256]{3,2,1,0:T(8,128)(2,1)S(1)} %bitcast.167), channel_id=1, replica_groups=mesh['zh'=4,'y'=8,'core'=2,'x'=4,'zl'=2] {'zh','core'}, dimensions={0} | all-to-all | bytes 786432 | tf_op jit(solution)/shard_map/all_to_all | solution.py:80
  35.4 1.3 stack.22
  36.7 7.2 %all-to-all-start.1 = ((bf16[8,8,48,256]{3,2,1,0:T(8,128)(2,1)}), bf16[8,8,48,256]{3,2,1,0:T(8,128)(2,1)S(1)}, u32[]{:S(2)}, u32[]{:S(2)}) async-start(bf16[8,8,48,256]{3,2,1,0:T(8,128)(2,1)} %stack.22), calls=%async_computation.1 | async-start | bytes 3145728 | tf_op jit(solution)/shard_map/all_to_all | solution.py:82
  45.1 1.5 multiply_reduce_fusion
  46.6 1.1 reshape.206
  47.7 1.2 copy.69
  49.1 13.7 %all-gather.1 = bf16[192,128]{1,0:T(8,128)(2,1)S(1)} all-gather(bf16[48,128]{1,0:T(8,128)(2,1)S(1)} %fusion.63), channel_id=3, replica_groups=mesh['zh'=4,'y'=8,'core'=2,'x'=4,'zl'=2] {'zh'}, dimensions={0}, use_global_device_ids=true | all-gather | bytes 61440 | tf_op jit(solution)/shard_map/all_gather | solution.py:86
  62.8 44.2 %all-gather.2 = bf16[64,48,128]{2,1,0:T(8,128)(2,1)} all-gather(bf16[4,48,128]{2,1,0:T(8,128)(2,1)S(1)} %bitcast.176), channel_id=4, replica_groups=mesh['zh'=4,'y'=8,'core'=2,'x'=4,'zl'=2] {'y','core'}, dimensions={0}, use_global_device_ids=true | all-gather | bytes 835584 | tf_op jit(solution)/shard_map/all_gather | solution.py:87
  107.0 2.2 collective-permute-start.2
  109.2 1.5 fusion.23
  110.8 2.1 collective-permute-start
  112.9 2.1 collective-permute-start.1
  115.0 2.5 %fusion.10 = (f32[128]{0:T(128)S(1)}, f32[2880,128]{1,0:T(8,128)}) fusion(bf16[128,2880]{0,1:T(8,128)(2,1)S(1)} %copy-done.1, f32[2880]{0:T(1024)S(1)} %mul.187, f32[128]{0:T(128)S(1)} %add_rsqrt_fusion, f32[2880]{0:T(1024)S(1)} %copy-done.13), kind=kLoop, calls=%fused_computation.17 | loop fusion | flops 1843072 | bytes 2235904 | tf_op jit(solution)/shard_map/reduce_sum | solution.py:169
  117.6 2.2 collective-permute-start.3
  119.8 1.2 pad.29
  121.0 1.0 copy.43
  122.1 2.1 reshape.213
  124.2 1.2 copy.62
  125.4 1.1 pad.30.clone
  126.4 2.5 %reshape.219 = f32[4,8,2,45,128]{4,3,2,1,0:T(8,128)} reshape(f32[2880,128]{1,0:T(8,128)} %get-tuple-element.9) | data formatting | bytes 2949120 | tf_op jit(solution)/shard_map/reshape | solution.py:35
  128.9 2.7 %copy.63 = f32[8,4,2,45,128]{4,3,2,1,0:T(8,128)} copy(f32[8,4,2,45,128]{4,3,2,0,1:T(8,128)} %bitcast.156) | data formatting | bytes 2949120
  131.6 2.7 %pad.31.clone = f32[8,4,2,48,128]{4,3,2,1,0:T(8,128)} pad(f32[8,4,2,45,128]{4,3,2,1,0:T(8,128)} %copy.63, f32[]{:T(128)} %constant.42.clone.1), padding=0_0x0_0x0_0x0_3x0_0 | pad | bytes 3047428 | tf_op jit(solution)/shard_map/jit(_pad)/pad | solution.py:36
  136.6 2.0 convolution_convert_fusion.4
  139.3 2.0 convolution_convert_fusion.2
  142.4 3.1 %fusion.106 = (f32[8,128]{1,0:T(8,128)}, f32[8,128,256]{2,1,0:T(8,128)}) fusion(bf16[8,64,128]{2,1,0:T(8,128)(2,1)} %bitcast.177, pred[128,256]{1,0:T(8,128)(4,1)} %fusion.43, bf16[128,128]{0,1:T(8,128)(2,1)S(1)} %fusion.23, bf16[128,128]{0,1:T(8,128)(2,1)S(1)} %collective-permute-done), kind=kOutput, calls=%fused_computation.137 | convolution fusion | flops 34668800 | bytes 1282048 | tf_op jit(solution)/shard_map/sub | solution.py:131
  145.4 7.1 %convolution_bitcast_fusion.2 = f32[64,256]{1,0:T(8,128)S(1)} fusion(bf16[8,64,128]{2,1,0:T(8,128)(2,1)} %bitcast.178, f32[8,128,256]{2,1,0:T(8,128)S(1)} %fusion.65, f32[8,128,256]{2,1,0:T(8,128)} %get-tuple-element.20, f32[8,128]{1,0:T(8,128)} %get-tuple-element.19), kind=kOutput, calls=%fused_computation.41 | convolution fusion | flops 35390720 | bytes 2297856 | tf_op jit(solution)/shard_map/hqk,hdq->dk/dot_general | solution.py:153
  152.6 3.6 %convolution_bitcast_fusion.1 = f32[64,256]{1,0:T(8,128)} fusion(bf16[8,64,128]{2,1,0:T(8,128)(2,1)} %bitcast.171, f32[8,128]{1,0:T(8,128)} %get-tuple-element.19, bf16[8,64,128]{2,1,0:T(8,128)(2,1)} %bitcast.179, pred[128,256]{1,0:T(8,128)(4,1)} %fusion.43, bf16[128,128]{0,1:T(8,128)(2,1)} %copy-done.15, bf16[128,128]{0,1:T(8,128)(2,1)} %copy-done.17), kind=kOutput, calls=%fused_computation.40 | convolution fusion | flops 68486400 | bytes 430080 | tf_op jit(solution)/shard_map/hqk,hdq->dk/dot_general | solution.py:147
  156.2 1.4 fusion.50
  157.5 1.5 collective-permute-start.4
  159.0 7.9 %fusion.21 = bf16[8,64,128]{2,1,0:T(8,128)(2,1)} fusion(f32[8,128,256]{2,1,0:T(8,128)S(1)} %fusion.65, bf16[128,128]{0,1:T(8,128)(2,1)} %copy-done.15, bf16[128,128]{0,1:T(8,128)(2,1)} %copy-done.17, f32[8,128,256]{2,1,0:T(8,128)} %get-tuple-element.20, f32[8,128]{1,0:T(8,128)} %get-tuple-element.19), kind=kOutput, calls=%fused_computation.33 | convolution fusion | flops 35521792 | bytes 2297856 | tf_op jit(solution)/shard_map/hqk,dk->hdq/dot_general | solution.py:151
  166.9 0.9 fusion.104
  168.9 1.1 fusion.52
  170.0 2.3 fusion.7
  172.4 0.9 pad_maximum_fusion
  173.4 4.7 %all-to-all-start.3 = ((bf16[8,400,128]{2,1,0:T(8,128)(2,1)}), bf16[8,400,128]{2,1,0:T(8,128)(2,1)S(1)}, u32[]{:S(2)}, u32[]{:S(2)}) async-start(bf16[8,400,128]{2,1,0:T(8,128)(2,1)} %pad_maximum_fusion), calls=%async_computation.3 | async-start | bytes 1638400 | tf_op jit(solution)/shard_map/all_to_all | solution.py:164
  178.1 3.1 %fusion.20 = bf16[8,64,128]{2,1,0:T(8,128)(2,1)S(1)} fusion(bf16[128,128]{0,1:T(8,128)(2,1)S(1)} %copy-done.16, bf16[128,128]{0,1:T(8,128)(2,1)} %copy-done.17, f32[8,128]{1,0:T(8,128)} %get-tuple-element.19, bf16[8,64,128]{2,1,0:T(8,128)(2,1)S(1)} %bitcast.180, pred[128,256]{1,0:T(8,128)(4,1)} %fusion.43), kind=kOutput, calls=%fused_computation.32 | convolution fusion | flops 68617472 | bytes 430080 | tf_op jit(solution)/shard_map/hqk,dk->hdq/dot_general | solution.py:134
  181.7 2.0 fusion.3
  183.7 1.0 copy.47
  184.7 6.2 %all-to-all-done.3 = bf16[8,400,128]{2,1,0:T(8,128)(2,1)S(1)} async-done(((bf16[8,400,128]{2,1,0:T(8,128)(2,1)}), bf16[8,400,128]{2,1,0:T(8,128)(2,1)S(1)}, u32[]{:S(2)}, u32[]{:S(2)}) %all-to-all-start.3) | async-done | bytes 819232 | tf_op jit(solution)/shard_map/all_to_all | solution.py:164
  190.9 5.2 %all-to-all-start.2 = ((bf16[8,384,128]{2,1,0:T(8,128)(2,1)}), bf16[8,384,128]{2,1,0:T(8,128)(2,1)S(1)}, u32[]{:S(2)}, u32[]{:S(2)}) async-start(bf16[8,384,128]{2,1,0:T(8,128)(2,1)} %bitcast.22), calls=%async_computation.2 | async-start | bytes 1572864 | tf_op jit(solution)/shard_map/all_to_all | solution.py:137
  196.7 10.7 %all-to-all-done.2 = bf16[8,384,128]{2,1,0:T(8,128)(2,1)S(1)} async-done(((bf16[8,384,128]{2,1,0:T(8,128)(2,1)}), bf16[8,384,128]{2,1,0:T(8,128)(2,1)S(1)}, u32[]{:S(2)}, u32[]{:S(2)}) %all-to-all-start.2) | async-done | bytes 786464 | tf_op jit(solution)/shard_map/all_to_all | solution.py:137
  208.1 3.4 %all-to-all-start.4 = ((f32[8,16,360]{2,1,0:T(8,128)}), f32[8,16,360]{2,1,0:T(8,128)S(1)}, u32[]{:S(2)}, u32[]{:S(2)}) async-start(f32[8,16,360]{2,1,0:T(8,128)} %broadcast_in_dim.34), calls=%async_computation.4 | async-start | bytes 393216 | tf_op jit(solution)/shard_map/all_to_all | solution.py:26
  211.8 11.0 %all-to-all-done.4 = f32[8,16,360]{2,1,0:T(8,128)S(1)} async-done(((f32[8,16,360]{2,1,0:T(8,128)}), f32[8,16,360]{2,1,0:T(8,128)S(1)}, u32[]{:S(2)}, u32[]{:S(2)}) %all-to-all-start.4) | async-done | bytes 184352 | tf_op jit(solution)/shard_map/all_to_all | solution.py:26
  223.4 4.5 %all-to-all-start.5 = ((f32[8,16,360]{2,1,0:T(8,128)}), f32[8,16,360]{2,1,0:T(8,128)S(1)}, u32[]{:S(2)}, u32[]{:S(2)}) async-start(f32[8,16,360]{2,1,0:T(8,128)} %broadcast_in_dim.35), calls=%async_computation.5 | async-start | bytes 393216 | tf_op jit(solution)/shard_map/all_to_all | solution.py:26
  227.9 1.0 fusion.22
  228.9 0.8 fusion.44
  229.7 8.8 %all-to-all-done.5 = f32[8,16,360]{2,1,0:T(8,128)S(1)} async-done(((f32[8,16,360]{2,1,0:T(8,128)}), f32[8,16,360]{2,1,0:T(8,128)S(1)}, u32[]{:S(2)}, u32[]{:S(2)}) %all-to-all-start.5) | async-done | bytes 184352 | tf_op jit(solution)/shard_map/all_to_all | solution.py:26
  (95 shorter events, 11.6 us)
Async XLA Ops:
  7.2 188.9 %copy-start = (bf16[16,2880]{1,0:T(8,128)(2,1)S(1)}, bf16[16,2880]{1,0:T(8,128)(2,1)}, u32[]{:S(2)}) copy-start(bf16[16,2880]{1,0:T(8,128)(2,1)} %param.18) | copy-start | bytes 276484
  36.7 8.0 %copy-start.1 = (bf16[128,2880]{0,1:T(8,128)(2,1)S(1)}, bf16[128,2880]{0,1:T(8,128)(2,1)}, u32[]{:S(2)}) copy-start(bf16[128,2880]{0,1:T(8,128)(2,1)} %param.11) | copy-start | bytes 2211844
  36.7 8.4 %copy-start.13 = (f32[2880]{0:T(1024)S(1)}, f32[2880]{0:T(1024)}, u32[]{:S(2)}) copy-start(f32[2880]{0:T(1024)} %param.12) | copy-start | bytes 34564
  36.7 8.4 %copy-start.14 = (f32[2880]{0:T(1024)S(1)}, f32[2880]{0:T(1024)}, u32[]{:S(2)}) copy-start(f32[2880]{0:T(1024)} %param.17) | copy-start | bytes 34564
  36.7 70.3 %all-to-all-start.1 = ((bf16[8,8,48,256]{3,2,1,0:T(8,128)(2,1)}), bf16[8,8,48,256]{3,2,1,0:T(8,128)(2,1)S(1)}, u32[]{:S(2)}, u32[]{:S(2)}) async-start(bf16[8,8,48,256]{3,2,1,0:T(8,128)(2,1)} %stack.22), calls=%async_computation.1 | async-start | bytes 3145728 | tf_op jit(solution)/shard_map/all_to_all | solution.py:82
  43.9 73.6 %all-gather.5.cloned.1.call-start = ((), (), s32[]{:S(2)}) async-start(), calls=%async_computation.6 | async-start | bytes 1769472 | tf_op jit(solution)/shard_map/all_gather | solution.py:84
  46.6 2.3 copy-start.18
  46.6 2.3 copy-start.19
  49.0 68.6 %copy-start.8 = (bf16[4,8,2,45,128]{4,3,2,0,1:T(8,128)(2,1)}, bf16[4,8,2,45,128]{4,3,2,0,1:T(8,128)(2,1)S(1)}, u32[]{:S(2)}) copy-start(bf16[4,8,2,45,128]{4,3,2,0,1:T(8,128)(2,1)S(1)} %copy.69) | copy-start | bytes 2211844
  49.0 63.9 %copy-start.21 = (s32[128]{0:T(128)S(1)}, s32[128]{0:T(128)}, u32[]{:S(2)}) copy-start(s32[128]{0:T(128)} %param.19) | copy-start | bytes 1540
  107.0 29.6 %collective-permute-start.2 = (bf16[3072,256]{1,0:T(8,128)(2,1)S(1)}, bf16[3072,256]{1,0:T(8,128)(2,1)}, u32[]{:S(2)}, u32[]{:S(2)}) collective-permute-start(bf16[3072,256]{1,0:T(8,128)(2,1)S(1)} %bitcast.146), channel_id=1, source_target_pairs={{0,8},{8,0},{1,9},{9,1},{2,10},{10,2},{3,11},{11,3},{4,12},{12,4},... | collective-permute-start | bytes 4718600 | tf_op jit(solution)/shard_map/ppermute | solution.py:90
  110.8 31.6 %copy-start.15 = (bf16[128,128]{0,1:T(8,128)(2,1)}, bf16[128,128]{0,1:T(8,128)(2,1)S(1)}, u32[]{:S(2)}) copy-start(bf16[128,128]{0,1:T(8,128)(2,1)S(1)} %fusion.23) | copy-start | bytes 98308
  110.8 30.6 %collective-permute-start = (bf16[128,128]{0,1:T(8,128)(2,1)S(1)}, bf16[128,128]{0,1:T(8,128)(2,1)S(1)}, u32[]{:S(2)}, u32[]{:S(2)}) collective-permute-start(bf16[128,128]{0,1:T(8,128)(2,1)S(1)} %fusion.23), channel_id=1, source_target_pairs={{0,8},{8,16},{16,24},{24,32},{32,40},{40,48},{48,56},{56,64},{64,7... | collective-permute-start | bytes 98312 | tf_op jit(solution)/shard_map/ppermute | solution.py:20
  112.9 21.5 %collective-permute-start.1 = (s32[128]{0:T(128)S(1)}, s32[128]{0:T(128)S(1)}, u32[]{:S(2)}, u32[]{:S(2)}) collective-permute-start(s32[128]{0:T(128)S(1)} %copy-done.21), channel_id=1, source_target_pairs={{0,8},{8,16},{16,24},{24,32},{32,40},{40,48},{48,56},{56,64},{64,7... | collective-permute-start | bytes 1544 | tf_op jit(solution)/shard_map/ppermute | solution.py:20
  117.6 3.5 %copy-start.9 = (bf16[64,48,128]{2,1,0:T(8,128)(2,1)S(1)}, bf16[64,48,128]{2,1,0:T(8,128)(2,1)}, u32[]{:S(2)}) copy-start(bf16[64,48,128]{2,1,0:T(8,128)(2,1)} %all-gather.2) | copy-start | bytes 2359300
  117.6 21.7 %collective-permute-start.3 = (bf16[3072,256]{1,0:T(8,128)(2,1)}, bf16[3072,256]{1,0:T(8,128)(2,1)}, u32[]{:S(2)}, u32[]{:S(2)}) collective-permute-start(bf16[3072,256]{1,0:T(8,128)(2,1)} %bitcast.153), channel_id=1, source_target_pairs={{0,8},{8,0},{1,9},{9,1},{2,10},{10,2},{3,11},{11,3},{4,12},{12,4},... | collective-permute-start | bytes 4718600 | tf_op jit(solution)/shard_map/ppermute | solution.py:91
  134.3 1.4 copy-start.2
  134.3 1.7 copy-start.3
  141.4 0.6 copy-start.10
  141.4 4.1 %copy-start.17 = (bf16[128,128]{0,1:T(8,128)(2,1)}, bf16[128,128]{0,1:T(8,128)(2,1)S(1)}, u32[]{:S(2)}) copy-start(bf16[128,128]{0,1:T(8,128)(2,1)S(1)} %collective-permute-done) | copy-start | bytes 98308
  157.5 10.8 %collective-permute-start.4 = (bf16[128,128]{1,0:T(8,128)(2,1)}, bf16[128,128]{1,0:T(8,128)(2,1)}, u32[]{:S(2)}, u32[]{:S(2)}) collective-permute-start(bf16[128,128]{1,0:T(8,128)(2,1)} %fusion.50), channel_id=1, source_target_pairs={{8,0},{16,8},{24,16},{32,24},{40,32},{48,40},{56,48},{64,56},{72,6... | collective-permute-start | bytes 98312 | tf_op jit(solution)/shard_map/ppermute | solution.py:20
  167.8 1.1 copy-start.7
  167.8 1.1 copy-start.11
  168.4 1.7 copy-start.5
  172.4 5.6 %copy-start.12 = (bf16[512,128]{1,0:T(8,128)(2,1)S(1)}, bf16[512,128]{1,0:T(8,128)(2,1)}, u32[]{:S(2)}) copy-start(bf16[512,128]{1,0:T(8,128)(2,1)} %pad_maximum_fusion.1) | copy-start | bytes 393220
  172.4 5.6 %copy-start.16 = (bf16[128,128]{0,1:T(8,128)(2,1)S(1)}, bf16[128,128]{0,1:T(8,128)(2,1)}, u32[]{:S(2)}) copy-start(bf16[128,128]{0,1:T(8,128)(2,1)} %copy-done.15) | copy-start | bytes 98308
  173.4 17.5 %all-to-all-start.3 = ((bf16[8,400,128]{2,1,0:T(8,128)(2,1)}), bf16[8,400,128]{2,1,0:T(8,128)(2,1)S(1)}, u32[]{:S(2)}, u32[]{:S(2)}) async-start(bf16[8,400,128]{2,1,0:T(8,128)(2,1)} %pad_maximum_fusion), calls=%async_computation.3 | async-start | bytes 1638400 | tf_op jit(solution)/shard_map/all_to_all | solution.py:164
  178.1 3.1 %copy-start.4 = (bf16[64,1,48,256]{3,2,1,0:T(8,128)(2,1)S(1)}, bf16[64,1,48,256]{3,2,1,0:T(8,128)(2,1)}, u32[]{:S(2)}) copy-start(bf16[64,1,48,256]{3,2,1,0:T(8,128)(2,1)} %all-gather.5.cloned.1.call-done) | copy-start | bytes 4718596
  183.7 12.4 %copy-start.6 = (bf16[128,2880]{0,1:T(8,128)(2,1)S(1)}, bf16[128,2880]{0,1:T(8,128)(2,1)}, u32[]{:S(2)}) copy-start(bf16[128,2880]{0,1:T(8,128)(2,1)} %param.21) | copy-start | bytes 2211844
  183.7 12.4 %copy-start.20 = (s32[128]{0:T(128)S(1)}, s32[128]{0:T(128)}, u32[]{:S(2)}) copy-start(s32[128]{0:T(128)} %param.20) | copy-start | bytes 1540
  190.9 16.5 %all-to-all-start.2 = ((bf16[8,384,128]{2,1,0:T(8,128)(2,1)}), bf16[8,384,128]{2,1,0:T(8,128)(2,1)S(1)}, u32[]{:S(2)}, u32[]{:S(2)}) async-start(bf16[8,384,128]{2,1,0:T(8,128)(2,1)} %bitcast.22), calls=%async_computation.2 | async-start | bytes 1572864 | tf_op jit(solution)/shard_map/all_to_all | solution.py:137
  208.1 14.7 %all-to-all-start.4 = ((f32[8,16,360]{2,1,0:T(8,128)}), f32[8,16,360]{2,1,0:T(8,128)S(1)}, u32[]{:S(2)}, u32[]{:S(2)}) async-start(f32[8,16,360]{2,1,0:T(8,128)} %broadcast_in_dim.34), calls=%async_computation.4 | async-start | bytes 393216 | tf_op jit(solution)/shard_map/all_to_all | solution.py:26
  223.4 15.1 %all-to-all-start.5 = ((f32[8,16,360]{2,1,0:T(8,128)}), f32[8,16,360]{2,1,0:T(8,128)S(1)}, u32[]{:S(2)}, u32[]{:S(2)}) async-start(f32[8,16,360]{2,1,0:T(8,128)} %broadcast_in_dim.35), calls=%async_computation.5 | async-start | bytes 393216 | tf_op jit(solution)/shard_map/all_to_all | solution.py:26
Sparse Core Ops, SparseCore 0:
  46.9 55.2 all-gather.4
